TPU v7x, 32 devices: a whole 2x2x4 slice. The times are simulated.
32 devices in a mesh: groups: 2 (over x), seq: 4 (over z), expert: 4 (over y, core).
Axes of the slice: x: 2, y: 2, z: 4, core: 2. Of those that a mesh axis runs over, the one named last changes fastest.
Arguments:
- q_lat: bfloat16 [512, 65536], P(('groups', 'seq'), 'expert'), parts along dimension 0, may hold values from -36 to 36
- q_rope: bfloat16 [512, 8192], P(('groups', 'seq'), 'expert'), parts along dimension 0, may hold values from -6 to 6
- cache_lat: bfloat16 [2048, 512], P(('groups', 'seq')), parts along dimension 0, may hold values from -7 to 7
- cache_rope: bfloat16 [2048, 64], P(('groups', 'seq')), parts along dimension 0, may hold values from -8 to 8
- tool_lat: bfloat16 [256, 512], P(('groups', 'seq')), parts along dimension 0, may hold values from -2.5 to 2.5
- tool_rope: bfloat16 [256, 64], P(('groups', 'seq')), parts along dimension 0, may hold values from -8 to 8
- offset: int32 [2], P('groups'), parts along dimension 0, may hold values from 512 to 736
- suf_lat: bfloat16 [512, 512], P(('groups', 'seq')), parts along dimension 0, may hold values from -6 to 6
- suf_rope: bfloat16 [512, 64], P(('groups', 'seq')), parts along dimension 0, may hold values from -8 to 8
- w_uv: bfloat16 [128, 512, 128], P('expert'), may hold values from -1 to 1
- w_out: bfloat16 [16384, 7168], P('expert', 'seq'), may hold values from -0.19921875 to 0.19921875
- resid: bfloat16 [512, 7168], P(('groups', 'expert'), 'seq'), parts along dimension 0, may hold values from -36 to 36
- routes: int32 [512, 2], P(('groups', 'expert')), parts along dimension 0, may hold values from 0 to 3, all different within a row; in each aligned block of 64 rows (0 to 63, 64 to 127, ...) at most 40 rows name the same one
- probs: float32 [512, 2], P(('groups', 'expert')), parts along dimension 0, may hold values from 0.1 to 1
- w_gate: bfloat16 [4, 7168, 1024], P('expert', None, 'seq'), may hold values from -0.0625 to 0.0625
- w_up: bfloat16 [4, 7168, 1024], P('expert', None, 'seq'), may hold values from -0.0625 to 0.0625
- w_down: bfloat16 [4, 1024, 7168], P('expert', 'seq'), may hold values from -0.1875 to 0.1875
Outputs:
- attn_residual: bfloat16 [512, 7168], P(('groups', 'expert'), 'seq'), parts along dimension 0
- expert_mix: bfloat16 [512, 7168], P(('groups', 'expert'), 'seq'), parts along dimension 0
There are 2 independent parts, one for each index of `groups`. A program takes and returns all parts, laid end to end along the dimension named above; an argument that names none is the same for every part. Nothing has to cross between parts.
Inputs may be any that keep to these rules, and one draw needn't show every extreme that they name: `routes`: within the rows of one device of the expert axis (64 rows in a row), no expert is named more than 40 times.
All inputs are finite; a program needn't handle non-finite values.
Results may differ from a plain program's by a relative error of at most 0.03.
Values may be sent and summed in bfloat16 or wider, within the bound.
No kernel may reach another device: no remote copies, remote signals or barrier semaphores. Data moves between devices by JAX's collectives and lax.ppermute only.
A program may use at most 128 MiB of HBM per device.

v0:
```python
import jax
import jax.numpy as jnp
from jax import lax
from jax.sharding import PartitionSpec as P

score_scale = 192.0 ** (-0.5)
floor_score = -1e30
norm_eps = 1e-06


def run_expert(tokens_in, w_gate, w_up, w_down):
    sources, count, width = tokens_in.shape
    rows = tokens_in.reshape(sources * count, width)
    gate = jnp.dot(rows, w_gate[0], preferred_element_type=jnp.float32)
    upper = jnp.dot(rows, w_up[0], preferred_element_type=jnp.float32)
    inner = (jax.nn.silu(gate) * upper).astype(jnp.bfloat16)
    partial_out = jnp.dot(inner, w_down[0], preferred_element_type=jnp.float32).reshape(
        sources, count, width
    )
    summed = lax.psum_scatter(
        partial_out.astype(jnp.bfloat16), "seq", scatter_dimension=2, tiled=True
    )
    return lax.all_to_all(summed, "expert", split_axis=0, concat_axis=0, tiled=True)


def on_device(
    q_lat,
    q_rope,
    cache_lat,
    cache_rope,
    tool_lat,
    tool_rope,
    offset,
    suf_lat,
    suf_rope,
    w_uv,
    w_out,
    resid,
    routes,
    probs,
    w_gate,
    w_up,
    w_down,
):
    seq_index = lax.axis_index("seq")
    ctx_dev = cache_lat.shape[0]
    query_dev = q_lat.shape[0]
    heads_dev, lat_width, value_width = w_uv.shape
    rope_width = cache_rope.shape[1]
    tool_all_lat, tool_all_rope = (
        lax.all_gather(tool_lat, "seq", axis=0, tiled=True),
        lax.all_gather(tool_rope, "seq", axis=0, tiled=True),
    )
    tool_len = tool_all_lat.shape[0]
    position = seq_index * ctx_dev + jnp.arange(ctx_dev, dtype=jnp.int32)
    shifted = position - offset[0]
    inside = (shifted >= 0) & (shifted < tool_len)
    safe = jnp.clip(shifted, 0, tool_len - 1)
    ctx_lat = jnp.where(inside[:, None], jnp.take(tool_all_lat, safe, axis=0), cache_lat)
    ctx_rope = jnp.where(inside[:, None], jnp.take(tool_all_rope, safe, axis=0), cache_rope)
    local_lat = jnp.concatenate([ctx_lat, suf_lat], axis=0)
    local_rope = jnp.concatenate([ctx_rope, suf_rope], axis=0)
    block_len = ctx_dev + query_dev
    query_rows = query_dev * heads_dev
    queries_lat = q_lat.reshape(query_rows, lat_width)
    queries_rope = q_rope.reshape(query_rows, rope_width)
    query_pos = seq_index * query_dev + jnp.arange(query_rows, dtype=jnp.int32) // heads_dev
    running_max = jnp.full((query_rows,), floor_score, jnp.float32)
    piece_lat = lax.all_gather(local_lat, "seq", axis=0, tiled=True)
    piece_rope = lax.all_gather(local_rope, "seq", axis=0, tiled=True)
    global_row = jnp.arange(piece_lat.shape[0], dtype=jnp.int32)
    within = global_row % block_len
    owner = global_row // block_len
    is_context = within < ctx_dev
    suffix_pos = owner * query_dev + within - ctx_dev
    visible = is_context[None, :] | (suffix_pos[None, :] <= query_pos[:, None])
    scores = jnp.einsum("qc,kc->qk", queries_lat, piece_lat, preferred_element_type=jnp.float32)
    scores = (
        scores
        + jnp.einsum("qc,kc->qk", queries_rope, piece_rope, preferred_element_type=jnp.float32)
    ) * score_scale
    scores = jnp.where(visible, scores, floor_score)
    new_max = jnp.maximum(running_max, jnp.max(scores, axis=1))
    weights = jnp.where(visible, jnp.exp(scores - new_max[:, None]), 0.0)
    new_total = jnp.sum(weights, axis=1)
    new_acc = jnp.dot(weights.astype(jnp.bfloat16), piece_lat, preferred_element_type=jnp.float32)
    latent_out = (
        (new_acc / new_total[:, None]).astype(jnp.bfloat16).reshape(query_dev, heads_dev, lat_width)
    )
    head_vals = jnp.einsum(
        "thc,hcv->thv", latent_out, w_uv, preferred_element_type=jnp.float32
    ).astype(jnp.bfloat16)
    head_vals = head_vals.reshape(query_dev, heads_dev * value_width)
    all_values = lax.all_gather(head_vals, "seq", axis=0, tiled=True)
    tok_dev = resid.shape[0]
    attn_sum = lax.psum_scatter(
        jnp.dot(all_values, w_out, preferred_element_type=jnp.float32).astype(jnp.bfloat16),
        "expert",
        scatter_dimension=0,
        tiled=True,
    ).astype(jnp.float32)
    attn_residual = (resid.astype(jnp.float32) + attn_sum).astype(jnp.bfloat16)
    expert_count = lax.axis_size("expert") * w_gate.shape[0]
    top_count = routes.shape[1]
    capacity = tok_dev * top_count * 5 // (4 * expert_count)
    flat_routes = routes.reshape(-1)
    one_hot = (flat_routes[:, None] == jnp.arange(expert_count, dtype=jnp.int32)[None, :]).astype(
        jnp.int32
    )
    earlier = jnp.cumsum(one_hot, axis=0) - one_hot
    slot = jnp.sum(earlier * one_hot, axis=1)
    target = (flat_routes * capacity + slot).reshape(tok_dev, top_count)
    slot_ids = jnp.arange(expert_count * capacity, dtype=jnp.int32)
    matches = slot_ids[:, None, None] == target[None, :, :]
    send_matrix = jnp.any(matches, axis=2).astype(jnp.bfloat16)
    route_weight = 2.5 * probs / jnp.sum(probs, axis=1, keepdims=True)
    gather_matrix = jnp.sum(jnp.where(matches, route_weight[None, :, :], 0.0), axis=2).T
    whole_stream = lax.all_gather(attn_residual, "seq", axis=1, tiled=True).astype(jnp.float32)
    normed = (
        whole_stream
        * lax.rsqrt(jnp.mean(whole_stream * whole_stream, axis=1, keepdims=True) + norm_eps)
    ).astype(jnp.bfloat16)
    outgoing = jnp.dot(send_matrix, normed, preferred_element_type=jnp.float32).astype(jnp.bfloat16)
    outgoing = outgoing.reshape(expert_count, capacity, normed.shape[1])
    returned = run_expert(
        lax.all_to_all(outgoing, "expert", split_axis=0, concat_axis=0, tiled=True),
        w_gate,
        w_up,
        w_down,
    )
    returned = returned.reshape(expert_count * capacity, returned.shape[2]).astype(jnp.float32)
    expert_mix = jnp.dot(
        gather_matrix, returned, precision=lax.Precision.HIGHEST, preferred_element_type=jnp.float32
    )
    return (attn_residual, expert_mix.astype(jnp.bfloat16))


def solution(mesh):
    placed = (
        P(("groups", "seq"), "expert"),
        P(("groups", "seq"), "expert"),
        P(("groups", "seq"), None),
        P(("groups", "seq"), None),
        P(("groups", "seq"), None),
        P(("groups", "seq"), None),
        P("groups"),
        P(("groups", "seq"), None),
        P(("groups", "seq"), None),
        P("expert", None, None),
        P("expert", "seq"),
        P(("groups", "expert"), "seq"),
        P(("groups", "expert"), None),
        P(("groups", "expert"), None),
        P("expert", None, "seq"),
        P("expert", None, "seq"),
        P("expert", "seq", None),
    )
    return jax.shard_map(
        on_device,
        mesh=mesh,
        in_specs=placed,
        out_specs=(P(("groups", "expert"), "seq"), P(("groups", "expert"), "seq")),
        check_vma=False,
    )
```

profile of v0, /device:TPU:0, one launch (start us, length us, event | category | flops | bytes accessed | tf_op | source)
XLA Modules:
  0.0 289.8 jit_solution(17597389861939251030)
XLA Ops:
  8.1 15.3 %all_gather.18 = bf16[128,512]{1,0:T(8,128)(2,1)S(1)} all-gather(bf16[32,512]{1,0:T(8,128)(2,1)} %param.21), channel_id=1, replica_groups=mesh['groups'=2,'seq'=4,'expert'=4] {'seq'}, dimensions={0}, use_global_device_ids=true | all-gather | bytes 163840 | tf_op jit(solution)/shard_map/all_gather | solution.py:51
  23.4 1.2 gather_fusion
  24.5 1.1 select_select_fusion
  25.7 1.6 pad_maximum_fusion
  27.4 2.4 reshape.119
  29.7 13.2 %all_gather.20 = bf16[128,64]{1,0:T(8,128)(2,1)S(1)} all-gather(bf16[32,64]{1,0:T(8,128)(2,1)S(1)} %copy-done.8), channel_id=1, replica_groups=mesh['groups'=2,'seq'=4,'expert'=4] {'seq'}, dimensions={0}, use_global_device_ids=true | all-gather | bytes 20480 | tf_op jit(solution)/shard_map/all_gather | solution.py:52
  44.3 15.6 %all-gather = bf16[4,320,64]{1,2,0:T(8,128)(2,1)S(1)} all-gather(bf16[1,320,64]{1,2,0:T(8,128)(2,1)S(1)} %copy.59), channel_id=1, replica_groups=mesh['groups'=2,'seq'=4,'expert'=4] {'seq'}, dimensions={0}, use_global_device_ids=true | all-gather | bytes 204800 | tf_op jit(solution)/shard_map/all_gather | solution.py:70
  60.8 3.9 %all-gather.4.cloned.1.call-done = bf16[1280,512]{1,0:T(8,128)(2,1)} async-done(((bf16[320,512]{1,0:T(8,128)(2,1)}), bf16[1280,512]{1,0:T(8,128)(2,1)}) %all-gather.4.cloned.1.call-update) | async-done | bytes 1310736 | tf_op jit(solution)/shard_map/all_gather | solution.py:69
  64.7 5.0 %fusion.51 = f32[1280,2048]{1,0:T(8,128)S(1)} fusion(bf16[1280,512]{1,0:T(8,128)(2,1)} %all-gather.4.cloned.1.call-done, bf16[2048,512]{1,0:T(8,128)(2,1)} %reshape.119), kind=kOutput, calls=%fused_computation.80 | convolution fusion | flops 2684354560 | bytes 13893632 | tf_op jit(solution)/shard_map/qc,kc->qk/dot_general | solution.py:77
  69.6 4.1 %fusion.50 = (f32[2048]{0:T(1024)S(1)}, f32[2048,1280]{0,1:T(8,128)S(1)}) fusion(f32[1280,2048]{1,0:T(8,128)S(1)} %fusion.51, bf16[1280,64]{0,1:T(8,128)(2,1)S(1)} %reshape.143, bf16[2048,64]{1,0:T(8,128)(2,1)S(1)} %reshape.120, s32[2048]{0:T(1024)S(1)} %fusion.40, s32[1280]{0:T(1024)S(1)} %fusion.38, pred[1280]{0:T(1024)(128)(4,1)S(1)} %fusion.45), kind=kOutput, calls=%fused_computation.79 | convolution fusion | flops 351270912 | bytes 21420288 | tf_op jit(solution)/shard_map/qc,kc->qk/dot_general | solution.py:80
  73.7 3.9 %fusion = f32[2048]{0:T(1024)S(1)} fusion(f32[2048,1280]{0,1:T(8,128)S(1)} %get-tuple-element.3, f32[2048]{0:T(1024)S(1)} %broadcast_maximum_fusion, s32[2048]{0:T(1024)S(1)} %fusion.40, s32[1280]{0:T(1024)S(1)} %fusion.38, pred[1280]{0:T(1024)(128)(4,1)S(1)} %fusion.45), kind=kLoop, calls=%fused_computation.7 | loop fusion | flops 13105152 | bytes 10516736 | tf_op jit(solution)/shard_map/reduce_sum | solution.py:85
  77.7 4.5 %divide_convert_fusion = bf16[2048,512]{1,0:T(8,128)(2,1)S(1)} fusion(f32[2048]{0:T(1024)S(1)} %fusion, bf16[1280,512]{1,0:T(8,128)(2,1)S(1)} %copy-done.13, f32[2048,1280]{0,1:T(8,128)S(1)} %get-tuple-element.3, f32[2048]{0:T(1024)S(1)} %broadcast_maximum_fusion, s32[2048]{0:T(1024)S(1)} %fusion.40, s32[1280]{0:T(1024)S(1)} %fusion.38, ...), kind=kOutput, calls=%fused_computation.15 | convolution fusion | flops 2699558912 | bytes 13924608 | tf_op jit(solution)/shard_map/dot_general | solution.py:86
  82.3 2.5 fusion.23
  85.8 44.8 %all-gather.6.cloned.1.call-done = bf16[256,4096]{1,0:T(8,128)(2,1)} async-done(((bf16[64,4096]{1,0:T(8,128)(2,1)}), bf16[256,4096]{1,0:T(8,128)(2,1)}) %all-gather.6.cloned.1.call-update) | async-done | bytes 2097168 | tf_op jit(solution)/shard_map/all_gather | solution.py:94
  130.6 10.7 %convolution_convert_fusion.2 = bf16[256,1792]{1,0:T(8,128)(2,1)} fusion(bf16[256,4096]{1,0:T(8,128)(2,1)} %all-gather.6.cloned.1.call-done, bf16[4096,1792]{1,0:T(8,128)(2,1)} %param.27), kind=kOutput, calls=%fused_computation.21 | convolution fusion | flops 3758555136 | bytes 17694720 | tf_op jit(solution)/shard_map/dot_general | solution.py:97
  142.7 21.6 %reduce-scatter.3.cloned.1.call-done = bf16[64,1792]{1,0:T(8,128)(2,1)} async-done(((bf16[256,1792]{1,0:T(8,128)(2,1)}), bf16[64,1792]{1,0:T(8,128)(2,1)}) %reduce-scatter.3.cloned.1.call-update) | async-done | bytes 229392 | tf_op jit(solution)/shard_map/reduce_scatter | solution.py:96
  165.3 21.0 %all_gather.23 = bf16[64,7168]{1,0:T(8,128)(2,1)S(1)} all-gather(bf16[64,1792]{1,0:T(8,128)(2,1)S(1)} %add_convert_fusion), channel_id=1, replica_groups=mesh['groups'=2,'seq'=4,'expert'=4] {'seq'}, dimensions={1}, use_global_device_ids=true | all-gather | bytes 1146880 | tf_op jit(solution)/shard_map/all_gather | solution.py:118
  187.5 30.4 %all_to_all.10 = bf16[4,40,7168]{2,1,0:T(8,128)(2,1)S(1)} all-to-all(bf16[4,40,7168]{2,1,0:T(8,128)(2,1)S(1)} %bitcast.51), channel_id=1, replica_groups=mesh['groups'=2,'seq'=4,'expert'=4] {'expert'}, dimensions={0} | all-to-all | bytes 4587520 | tf_op jit(solution)/shard_map/all_to_all | solution.py:126
  218.6 1.3 copy-done.11
  220.7 1.3 copy-done.12
  221.9 2.2 convolution_convert_fusion
  224.1 45.3 %reduce-scatter.5.cloned.1.call-done = bf16[4,40,1792]{2,1,0:T(8,128)(2,1)} async-done(((bf16[4,40,7168]{2,1,0:T(8,128)(2,1)}), bf16[4,40,1792]{2,1,0:T(8,128)(2,1)}) %reduce-scatter.5.cloned.1.call-update) | async-done | bytes 573456 | tf_op jit(solution)/shard_map/reduce_scatter | solution.py:20
  269.4 3.5 %all-to-all-start.1 = ((bf16[4,40,1792]{2,1,0:T(8,128)(2,1)}), bf16[4,40,1792]{2,1,0:T(8,128)(2,1)S(1)}, u32[]{:S(2)}, u32[]{:S(2)}) async-start(bf16[4,40,1792]{2,1,0:T(8,128)(2,1)} %reduce-scatter.5.cloned.1.call-done), calls=%async_computation.3 | async-start | bytes 1146880 | tf_op jit(solution)/shard_map/all_to_all | solution.py:23
  273.1 9.2 %all-to-all-done.1 = bf16[4,40,1792]{2,1,0:T(8,128)(2,1)S(1)} async-done(((bf16[4,40,1792]{2,1,0:T(8,128)(2,1)}), bf16[4,40,1792]{2,1,0:T(8,128)(2,1)S(1)}, u32[]{:S(2)}, u32[]{:S(2)}) %all-to-all-start.1) | async-done | bytes 573472 | tf_op jit(solution)/shard_map/all_to_all | solution.py:23
  (69 shorter events, 9.4 us)
Async XLA Ops:
  7.2 20.2 %copy-start.2 = (bf16[64,16384]{1,0:T(8,128)(2,1)S(1)}, bf16[64,16384]{1,0:T(8,128)(2,1)}, u32[]{:S(2)}) copy-start(bf16[64,16384]{1,0:T(8,128)(2,1)} %param.17) | copy-start | bytes 6291460
  7.2 57.5 %all-gather.4.cloned.1.call-start = ((), (), s32[]{:S(2)}) async-start(), calls=%async_computation.4 | async-start | bytes 1638400 | tf_op jit(solution)/shard_map/all_gather | solution.py:69
  23.4 6.4 %copy-start.8 = (bf16[32,64]{1,0:T(8,128)(2,1)S(1)}, bf16[32,64]{1,0:T(8,128)(2,1)}, u32[]{:S(2)}) copy-start(bf16[32,64]{1,0:T(8,128)(2,1)} %param.22) | copy-start | bytes 12292
  24.5 19.3 %copy-start.6 = (bf16[256,64]{0,1:T(8,128)(2,1)S(1)}, bf16[256,64]{0,1:T(8,128)(2,1)}, u32[]{:S(2)}) copy-start(bf16[256,64]{0,1:T(8,128)(2,1)} %param.20) | copy-start | bytes 98308
  24.5 19.6 %copy-start.7 = (bf16[64,64]{1,0:T(8,128)(2,1)S(1)}, bf16[64,64]{1,0:T(8,128)(2,1)}, u32[]{:S(2)}) copy-start(bf16[64,64]{1,0:T(8,128)(2,1)} %param.25) | copy-start | bytes 24580
  25.6 34.5 %copy-start.4 = (bf16[64,2048]{1,0:T(8,128)(2,1)S(1)}, bf16[64,2048]{1,0:T(8,128)(2,1)}, u32[]{:S(2)}) copy-start(bf16[64,2048]{1,0:T(8,128)(2,1)} %param.18) | copy-start | bytes 786436
  27.3 103.3 %all-gather.6.cloned.1.call-start = ((), (), s32[]{:S(2)}) async-start(), calls=%async_computation.5 | async-start | bytes 2621440 | tf_op jit(solution)/shard_map/all_gather | solution.py:94
  73.7 4.0 %copy-start.13 = (bf16[1280,512]{1,0:T(8,128)(2,1)S(1)}, bf16[1280,512]{1,0:T(8,128)(2,1)}, u32[]{:S(2)}) copy-start(bf16[1280,512]{1,0:T(8,128)(2,1)} %all-gather.4.cloned.1.call-done) | copy-start | bytes 3932164
  77.7 4.6 %copy-start = (bf16[32,512,128]{2,1,0:T(8,128)(2,1)S(1)}, bf16[32,512,128]{2,1,0:T(8,128)(2,1)}, u32[]{:S(2)}) copy-start(bf16[32,512,128]{2,1,0:T(8,128)(2,1)} %param.26) | copy-start | bytes 12582916
  85.7 55.9 %copy-start.9 = (s32[64,2]{0,1:T(2,128)S(1)}, s32[64,2]{0,1:T(2,128)}, u32[]{:S(2)}) copy-start(s32[64,2]{0,1:T(2,128)} %param.29) | copy-start | bytes 1540
  85.7 78.6 %copy-start.5 = (bf16[64,1792]{1,0:T(8,128)(2,1)S(1)}, bf16[64,1792]{1,0:T(8,128)(2,1)}, u32[]{:S(2)}) copy-start(bf16[64,1792]{1,0:T(8,128)(2,1)} %param.28) | copy-start | bytes 688132
  85.7 78.6 %reduce-scatter.3.cloned.1.call-start = ((), (), s32[]{:S(2)}) async-start(), calls=%async_computation.6 | async-start | bytes 1146880 | tf_op jit(solution)/shard_map/reduce_scatter | solution.py:96
  141.4 128.1 %reduce-scatter.5.cloned.1.call-start = ((), (), s32[]{:S(2)}) async-start(), calls=%async_computation.7 | async-start | bytes 2867200 | tf_op jit(solution)/shard_map/reduce_scatter | solution.py:20
  165.3 52.5 %copy-start.3 = (bf16[64,1792]{1,0:T(8,128)(2,1)}, bf16[64,1792]{1,0:T(8,128)(2,1)S(1)}, u32[]{:S(2)}) copy-start(bf16[64,1792]{1,0:T(8,128)(2,1)S(1)} %add_convert_fusion) | copy-start | bytes 688132
  186.6 31.2 %copy-start.1 = (bf16[1,7168,256]{2,1,0:T(8,128)(2,1)S(1)}, bf16[1,7168,256]{2,1,0:T(8,128)(2,1)}, u32[]{:S(2)}) copy-start(bf16[1,7168,256]{2,1,0:T(8,128)(2,1)} %param.31) | copy-start | bytes 11010052
  217.8 2.0 copy-start.11
  219.9 2.0 copy-start.12
  221.9 51.0 %copy-start.10 = (f32[64,2]{0,1:T(2,128)S(1)}, f32[64,2]{0,1:T(2,128)}, u32[]{:S(2)}) copy-start(f32[64,2]{0,1:T(2,128)} %param.30) | copy-start | bytes 1540
  269.4 12.8 %all-to-all-start.1 = ((bf16[4,40,1792]{2,1,0:T(8,128)(2,1)}), bf16[4,40,1792]{2,1,0:T(8,128)(2,1)S(1)}, u32[]{:S(2)}, u32[]{:S(2)}) async-start(bf16[4,40,1792]{2,1,0:T(8,128)(2,1)} %reduce-scatter.5.cloned.1.call-done), calls=%async_computation.3 | async-start | bytes 1146880 | tf_op jit(solution)/shard_map/all_to_all | solution.py:23
Sparse Core Ops, SparseCore 0:
  27.4 37.1 all-gather.3
  85.8 44.7 all-gather.5
  141.5 22.7 reduce-scatter.2
  224.3 45.1 reduce-scatter.4
where the time goes:
time: 290 us
  waiting for transfers between devices  125 us (43%)
  blocking collectives  95.5 us (33%)
  matrix products  32.4 us (11%)
  between operations  14.9 us (5%)
  local copies, waits for them, and re-layouts  9.37 us (3%)
  other arithmetic  8.86 us (3%)
  starting transfers between devices  3.86 us (1%)
    reduce_scatter x1, waiting for transfers between devices, run_expert(): lax.psum_scatter(partial_out.astype(jnp.bfloat16), 'seq', scatter_dimensi...  45.3 us
    all_gather x1, waiting for transfers between devices, on_device(): all_values = lax.all_gather(head_vals, 'seq', axis=0, tiled=True)  44.8 us
    all_to_all x1, blocking collectives, on_device(): lax.all_to_all(outgoing, 'expert', split_axis=0, concat_axis=0, tiled=True)  30.4 us
    reduce_scatter x1, waiting for transfers between devices, on_device(): lax.psum_scatter(jnp.dot(all_values, w_out, preferred_element_type=jnp.fl...  21.6 us
    all_gather x1, blocking collectives, on_device(): lax.all_gather(attn_residual, 'seq', axis=1, tiled=True).astype(jnp.float32)  21 us
    all_gather x1, blocking collectives, on_device(): piece_rope = lax.all_gather(local_rope, 'seq', axis=0, tiled=True)  15.6 us
    all_gather x1, blocking collectives, on_device(): lax.all_gather(tool_lat, 'seq', axis=0, tiled=True)  15.3 us
    all_gather x1, blocking collectives, on_device(): lax.all_gather(tool_rope, 'seq', axis=0, tiled=True)  13.2 us
  transfers between devices with their start and end apart: 5, of which 5 were waited for; matrix products, arithmetic and copies ran while one was open for 2% of the time, Pallas kernels for 0%

commit v1 on v0

--- a/solution.py
+++ b/solution.py
@@ -91,7 +91,22 @@
         "thc,hcv->thv", latent_out, w_uv, preferred_element_type=jnp.float32
     ).astype(jnp.bfloat16)
     head_vals = head_vals.reshape(query_dev, heads_dev * value_width)
-    all_values = lax.all_gather(head_vals, "seq", axis=0, tiled=True)
+    ways, here, step = (lax.axis_size("seq"), lax.axis_index("seq"), head_vals.shape[0])
+    lengths = [n * ways if d == 0 else n for d, n in enumerate(head_vals.shape)]
+    all_values = lax.dynamic_update_slice_in_dim(
+        jnp.zeros(lengths, head_vals.dtype), head_vals, here * step, axis=0
+    )
+    going_up = going_down = head_vals
+    for far in range(1, ways // 2 + 1):
+        going_up = lax.ppermute(going_up, "seq", [(d, (d + 1) % ways) for d in range(ways)])
+        all_values = lax.dynamic_update_slice_in_dim(
+            all_values, going_up, (here - far) % ways * step, axis=0
+        )
+        if 2 * far < ways:
+            going_down = lax.ppermute(going_down, "seq", [(d, (d - 1) % ways) for d in range(ways)])
+            all_values = lax.dynamic_update_slice_in_dim(
+                all_values, going_down, (here + far) % ways * step, axis=0
+            )
     tok_dev = resid.shape[0]
     attn_sum = lax.psum_scatter(
         jnp.dot(all_values, w_out, preferred_element_type=jnp.float32).astype(jnp.bfloat16),

time: 290 us -> 277 us (0.955)
  waiting for transfers between devices: 125 us -> 113 us
  starting transfers between devices: 3.86 us -> 7.48 us
  matrix products: 32.4 us -> 29.3 us
    all_gather x1 -> x0, waiting for transfers between devices: 44.8 us -> none  [on_device(): all_values = lax.all_gather(head_vals, 'seq', axis=0, tiled=True)]
    ppermute x0 -> x3, waiting for transfers between devices: none -> 32.8 us  [the longest x2 23 us: on_device(): lax.ppermute(going_up, 'seq', [(d, (d + 1) % ways) for d in range(ways)])]
    ppermute x0 -> x3, starting transfers between devices: none -> 3.88 us  [the longest x1 2.91 us: on_device(): lax.ppermute(going_down, 'seq', [(d, (d - 1) % ways) for d in range(ways)])]
  transfers between devices with their start and end apart: 5 -> 7, of which waited for: 5 -> 7; matrix products, arithmetic and copies ran while one was open for 2% -> 2% of each run, Pallas kernels for 0% -> 0%
where the time goes in v1:
time: 277 us
  waiting for transfers between devices  113 us (41%)
  blocking collectives  96 us (35%)
  matrix products  29.3 us (11%)
  between operations  15 us (5%)
  local copies, waits for them, and re-layouts  8.99 us (3%)
  starting transfers between devices  7.48 us (3%)
  other arithmetic  6.98 us (3%)
    reduce_scatter x1, waiting for transfers between devices, run_expert(): lax.psum_scatter(partial_out.astype(jnp.bfloat16), 'seq', scatter_dimensi...  45.3 us
    all_to_all x1, blocking collectives, on_device(): lax.all_to_all(outgoing, 'expert', split_axis=0, concat_axis=0, tiled=True)  30.5 us
    ppermute x2, waiting for transfers between devices, on_device(): lax.ppermute(going_up, 'seq', [(d, (d + 1) % ways) for d in range(ways)])  23 us
    reduce_scatter x1, waiting for transfers between devices, on_device(): lax.psum_scatter(jnp.dot(all_values, w_out, preferred_element_type=jnp.fl...  21.8 us
    all_gather x1, blocking collectives, on_device(): lax.all_gather(attn_residual, 'seq', axis=1, tiled=True).astype(jnp.float32)  21.2 us
    all_gather x1, blocking collectives, on_device(): piece_rope = lax.all_gather(local_rope, 'seq', axis=0, tiled=True)  15.5 us
    all_gather x1, blocking collectives, on_device(): lax.all_gather(tool_lat, 'seq', axis=0, tiled=True)  15.3 us
    all_gather x1, blocking collectives, on_device(): lax.all_gather(tool_rope, 'seq', axis=0, tiled=True)  13.4 us
  transfers between devices with their start and end apart: 7, of which 7 were waited for; matrix products, arithmetic and copies ran while one was open for 2% of the time, Pallas kernels for 0%

profile of v1, /device:TPU:0, one launch (start us, length us, event | category | flops | bytes accessed | tf_op | source)
XLA Modules:
  0.0 276.6 jit_solution(13854912408070986237)
XLA Ops:
  8.1 15.3 %all_gather.15 = bf16[128,512]{1,0:T(8,128)(2,1)S(1)} all-gather(bf16[32,512]{1,0:T(8,128)(2,1)} %param.21), channel_id=1, replica_groups=mesh['groups'=2,'seq'=4,'expert'=4] {'seq'}, dimensions={0}, use_global_device_ids=true | all-gather | bytes 163840 | tf_op jit(solution)/shard_map/all_gather | solution.py:51
  25.6 2.3 reshape.119
  28.0 13.4 %all_gather.17 = bf16[128,64]{1,0:T(8,128)(2,1)S(1)} all-gather(bf16[32,64]{1,0:T(8,128)(2,1)S(1)} %copy-done.11), channel_id=1, replica_groups=mesh['groups'=2,'seq'=4,'expert'=4] {'seq'}, dimensions={0}, use_global_device_ids=true | all-gather | bytes 20480 | tf_op jit(solution)/shard_map/all_gather | solution.py:52
  42.7 15.5 %all-gather = bf16[4,320,64]{1,2,0:T(8,128)(2,1)S(1)} all-gather(bf16[1,320,64]{1,2,0:T(8,128)(2,1)S(1)} %copy.59), channel_id=1, replica_groups=mesh['groups'=2,'seq'=4,'expert'=4] {'seq'}, dimensions={0}, use_global_device_ids=true | all-gather | bytes 204800 | tf_op jit(solution)/shard_map/all_gather | solution.py:70
  59.1 3.7 %all-gather.3.cloned.1.call-done = bf16[1280,512]{1,0:T(8,128)(2,1)} async-done(((bf16[320,512]{1,0:T(8,128)(2,1)}), bf16[1280,512]{1,0:T(8,128)(2,1)}) %all-gather.3.cloned.1.call-update) | async-done | bytes 1310736 | tf_op jit(solution)/shard_map/all_gather | solution.py:69
  62.9 4.3 %fusion.51 = f32[1280,2048]{1,0:T(8,128)S(1)} fusion(bf16[1280,512]{1,0:T(8,128)(2,1)} %all-gather.3.cloned.1.call-done, bf16[2048,512]{1,0:T(8,128)(2,1)S(1)} %copy-done.3), kind=kOutput, calls=%fused_computation.84 | convolution fusion | flops 2684354560 | bytes 13893632 | tf_op jit(solution)/shard_map/qc,kc->qk/dot_general | solution.py:77
  67.1 4.1 %fusion.50 = (f32[2048]{0:T(1024)S(1)}, f32[2048,1280]{0,1:T(8,128)S(1)}) fusion(f32[1280,2048]{1,0:T(8,128)S(1)} %fusion.51, bf16[1280,64]{0,1:T(8,128)(2,1)S(1)} %reshape.143, bf16[2048,64]{1,0:T(8,128)(2,1)S(1)} %reshape.120, s32[2048]{0:T(1024)S(1)} %fusion.40, s32[1280]{0:T(1024)S(1)} %fusion.38, pred[1280]{0:T(1024)(128)(4,1)S(1)} %fusion.45), kind=kOutput, calls=%fused_computation.83 | convolution fusion | flops 351270912 | bytes 21420288 | tf_op jit(solution)/shard_map/qc,kc->qk/dot_general | solution.py:80
  71.2 3.9 %fusion = f32[2048]{0:T(1024)S(1)} fusion(f32[2048,1280]{0,1:T(8,128)S(1)} %get-tuple-element.3, f32[2048]{0:T(1024)S(1)} %broadcast_maximum_fusion, s32[2048]{0:T(1024)S(1)} %fusion.40, s32[1280]{0:T(1024)S(1)} %fusion.38, pred[1280]{0:T(1024)(128)(4,1)S(1)} %fusion.45), kind=kLoop, calls=%fused_computation.7 | loop fusion | flops 13105152 | bytes 10516736 | tf_op jit(solution)/shard_map/reduce_sum | solution.py:85
  75.2 4.5 %divide_convert_fusion = bf16[2048,512]{1,0:T(8,128)(2,1)S(1)} fusion(f32[2048]{0:T(1024)S(1)} %fusion, bf16[1280,512]{1,0:T(8,128)(2,1)S(1)} %copy-done.16, f32[2048,1280]{0,1:T(8,128)S(1)} %get-tuple-element.3, f32[2048]{0:T(1024)S(1)} %broadcast_maximum_fusion, s32[2048]{0:T(1024)S(1)} %fusion.40, s32[1280]{0:T(1024)S(1)} %fusion.38, ...), kind=kOutput, calls=%fused_computation.15 | convolution fusion | flops 2699558912 | bytes 13924608 | tf_op jit(solution)/shard_map/dot_general | solution.py:86
  79.7 2.5 fusion.23
  83.3 2.9 %collective-permute-start.1 = (bf16[64,4096]{1,0:T(8,128)(2,1)S(1)}, bf16[64,4096]{1,0:T(8,128)(2,1)S(1)}, u32[]{:S(2)}, u32[]{:S(2)}) collective-permute-start(bf16[64,4096]{1,0:T(8,128)(2,1)S(1)} %bitcast.57), channel_id=1, source_target_pairs={{0,12},{4,0},{8,4},{12,8},{1,13},{5,1},{9,5},{13,9},{2,14},{6,2},{... | collective-permute-start | bytes 1572872 | tf_op jit(solution)/shard_map/ppermute | solution.py:106
  86.6 12.4 %collective-permute-done = bf16[64,4096]{1,0:T(8,128)(2,1)S(1)} collective-permute-done((bf16[64,4096]{1,0:T(8,128)(2,1)S(1)}, bf16[64,4096]{1,0:T(8,128)(2,1)S(1)}, u32[]{:S(2)}, u32[]{:S(2)}) %collective-permute-start) | collective-permute-done | bytes 524320 | tf_op jit(solution)/shard_map/ppermute | solution.py:101
  99.0 9.8 %collective-permute-done.1 = bf16[64,4096]{1,0:T(8,128)(2,1)S(1)} collective-permute-done((bf16[64,4096]{1,0:T(8,128)(2,1)S(1)}, bf16[64,4096]{1,0:T(8,128)(2,1)S(1)}, u32[]{:S(2)}, u32[]{:S(2)}) %collective-permute-start.1) | collective-permute-done | bytes 524320 | tf_op jit(solution)/shard_map/ppermute | solution.py:106
  108.9 10.6 %collective-permute-done.2 = bf16[64,4096]{1,0:T(8,128)(2,1)S(1)} collective-permute-done((bf16[64,4096]{1,0:T(8,128)(2,1)S(1)}, bf16[64,4096]{1,0:T(8,128)(2,1)S(1)}, u32[]{:S(2)}, u32[]{:S(2)}) %collective-permute-start.2) | collective-permute-done | bytes 524320 | tf_op jit(solution)/shard_map/ppermute | solution.py:101
  119.5 8.3 %convolution_convert_fusion.2 = bf16[256,1792]{1,0:T(8,128)(2,1)} fusion(bf16[256,4096]{1,0:T(8,128)(2,1)S(1)} %constant_dynamic-update-slice_fusion, bf16[4096,1792]{1,0:T(8,128)(2,1)} %param.27), kind=kOutput, calls=%fused_computation.21 | convolution fusion | flops 3758555136 | bytes 17694720 | tf_op jit(solution)/shard_map/dot_general | solution.py:112
  129.0 21.8 %reduce-scatter.3.cloned.1.call-done = bf16[64,1792]{1,0:T(8,128)(2,1)} async-done(((bf16[256,1792]{1,0:T(8,128)(2,1)}), bf16[64,1792]{1,0:T(8,128)(2,1)}) %reduce-scatter.3.cloned.1.call-update) | async-done | bytes 229392 | tf_op jit(solution)/shard_map/reduce_scatter | solution.py:111
  151.8 21.2 %all_gather.19 = bf16[64,7168]{1,0:T(8,128)(2,1)S(1)} all-gather(bf16[64,1792]{1,0:T(8,128)(2,1)S(1)} %add_convert_fusion), channel_id=1, replica_groups=mesh['groups'=2,'seq'=4,'expert'=4] {'seq'}, dimensions={1}, use_global_device_ids=true | all-gather | bytes 1146880 | tf_op jit(solution)/shard_map/all_gather | solution.py:133
  174.2 30.5 %all_to_all.10 = bf16[4,40,7168]{2,1,0:T(8,128)(2,1)S(1)} all-to-all(bf16[4,40,7168]{2,1,0:T(8,128)(2,1)S(1)} %bitcast.53), channel_id=1, replica_groups=mesh['groups'=2,'seq'=4,'expert'=4] {'expert'}, dimensions={0} | all-to-all | bytes 4587520 | tf_op jit(solution)/shard_map/all_to_all | solution.py:141
  205.4 1.3 copy-done.14
  207.5 1.3 copy-done.15
  208.7 2.2 convolution_convert_fusion
  210.9 45.3 %reduce-scatter.5.cloned.1.call-done = bf16[4,40,1792]{2,1,0:T(8,128)(2,1)} async-done(((bf16[4,40,7168]{2,1,0:T(8,128)(2,1)}), bf16[4,40,1792]{2,1,0:T(8,128)(2,1)}) %reduce-scatter.5.cloned.1.call-update) | async-done | bytes 573456 | tf_op jit(solution)/shard_map/reduce_scatter | solution.py:20
  256.2 3.5 %all-to-all-start.1 = ((bf16[4,40,1792]{2,1,0:T(8,128)(2,1)}), bf16[4,40,1792]{2,1,0:T(8,128)(2,1)S(1)}, u32[]{:S(2)}, u32[]{:S(2)}) async-start(bf16[4,40,1792]{2,1,0:T(8,128)(2,1)} %reduce-scatter.5.cloned.1.call-done), calls=%async_computation.3 | async-start | bytes 1146880 | tf_op jit(solution)/shard_map/all_to_all | solution.py:23
  259.9 9.2 %all-to-all-done.1 = bf16[4,40,1792]{2,1,0:T(8,128)(2,1)S(1)} async-done(((bf16[4,40,1792]{2,1,0:T(8,128)(2,1)}), bf16[4,40,1792]{2,1,0:T(8,128)(2,1)S(1)}, u32[]{:S(2)}, u32[]{:S(2)}) %all-to-all-start.1) | async-done | bytes 573472 | tf_op jit(solution)/shard_map/all_to_all | solution.py:23
  (83 shorter events, 11.8 us)
Async XLA Ops:
  7.2 17.4 %copy-start.6 = (bf16[256,512]{1,0:T(8,128)(2,1)S(1)}, bf16[256,512]{1,0:T(8,128)(2,1)}, u32[]{:S(2)}) copy-start(bf16[256,512]{1,0:T(8,128)(2,1)} %param.19) | copy-start | bytes 786436
  7.2 17.5 %copy-start.8 = (bf16[64,512]{1,0:T(8,128)(2,1)S(1)}, bf16[64,512]{1,0:T(8,128)(2,1)}, u32[]{:S(2)}) copy-start(bf16[64,512]{1,0:T(8,128)(2,1)} %param.24) | copy-start | bytes 196612
  7.2 18.4 %copy-start.2 = (bf16[64,16384]{1,0:T(8,128)(2,1)S(1)}, bf16[64,16384]{1,0:T(8,128)(2,1)}, u32[]{:S(2)}) copy-start(bf16[64,16384]{1,0:T(8,128)(2,1)} %param.17) | copy-start | bytes 6291460
  7.2 55.7 %all-gather.3.cloned.1.call-start = ((), (), s32[]{:S(2)}) async-start(), calls=%async_computation.4 | async-start | bytes 1638400 | tf_op jit(solution)/shard_map/all_gather | solution.py:69
  24.7 3.3 %copy-start.11 = (bf16[32,64]{1,0:T(8,128)(2,1)S(1)}, bf16[32,64]{1,0:T(8,128)(2,1)}, u32[]{:S(2)}) copy-start(bf16[32,64]{1,0:T(8,128)(2,1)} %param.22) | copy-start | bytes 12292
  25.5 16.8 %copy-start.9 = (bf16[256,64]{0,1:T(8,128)(2,1)S(1)}, bf16[256,64]{0,1:T(8,128)(2,1)}, u32[]{:S(2)}) copy-start(bf16[256,64]{0,1:T(8,128)(2,1)} %param.20) | copy-start | bytes 98308
  25.5 17.0 %copy-start.10 = (bf16[64,64]{1,0:T(8,128)(2,1)S(1)}, bf16[64,64]{1,0:T(8,128)(2,1)}, u32[]{:S(2)}) copy-start(bf16[64,64]{1,0:T(8,128)(2,1)} %param.25) | copy-start | bytes 24580
  25.5 125.2 %reduce-scatter.3.cloned.1.call-start = ((), (), s32[]{:S(2)}) async-start(), calls=%async_computation.5 | async-start | bytes 1146880 | tf_op jit(solution)/shard_map/reduce_scatter | solution.py:111
  25.6 32.9 %copy-start.5 = (bf16[64,2048]{1,0:T(8,128)(2,1)S(1)}, bf16[64,2048]{1,0:T(8,128)(2,1)}, u32[]{:S(2)}) copy-start(bf16[64,2048]{1,0:T(8,128)(2,1)} %param.18) | copy-start | bytes 786436
  28.0 34.9 %copy-start.3 = (bf16[2048,512]{1,0:T(8,128)(2,1)S(1)}, bf16[2048,512]{1,0:T(8,128)(2,1)}, u32[]{:S(2)}) copy-start(bf16[2048,512]{1,0:T(8,128)(2,1)} %reshape.119) | copy-start | bytes 6291460
  71.2 3.9 %copy-start.16 = (bf16[1280,512]{1,0:T(8,128)(2,1)S(1)}, bf16[1280,512]{1,0:T(8,128)(2,1)}, u32[]{:S(2)}) copy-start(bf16[1280,512]{1,0:T(8,128)(2,1)} %all-gather.3.cloned.1.call-done) | copy-start | bytes 3932164
  75.2 4.5 %copy-start = (bf16[32,512,128]{2,1,0:T(8,128)(2,1)S(1)}, bf16[32,512,128]{2,1,0:T(8,128)(2,1)}, u32[]{:S(2)}) copy-start(bf16[32,512,128]{2,1,0:T(8,128)(2,1)} %param.26) | copy-start | bytes 12582916
  82.3 16.7 %collective-permute-start = (bf16[64,4096]{1,0:T(8,128)(2,1)S(1)}, bf16[64,4096]{1,0:T(8,128)(2,1)S(1)}, u32[]{:S(2)}, u32[]{:S(2)}) collective-permute-start(bf16[64,4096]{1,0:T(8,128)(2,1)S(1)} %bitcast.56), channel_id=1, source_target_pairs={{0,4},{4,8},{8,12},{12,0},{1,5},{5,9},{9,13},{13,1},{2,6},{6,10},{... | collective-permute-start | bytes 1572872 | tf_op jit(solution)/shard_map/ppermute | solution.py:101
  83.3 25.6 %collective-permute-start.1 = (bf16[64,4096]{1,0:T(8,128)(2,1)S(1)}, bf16[64,4096]{1,0:T(8,128)(2,1)S(1)}, u32[]{:S(2)}, u32[]{:S(2)}) collective-permute-start(bf16[64,4096]{1,0:T(8,128)(2,1)S(1)} %bitcast.57), channel_id=1, source_target_pairs={{0,12},{4,0},{8,4},{12,8},{1,13},{5,1},{9,5},{13,9},{2,14},{6,2},{... | collective-permute-start | bytes 1572872 | tf_op jit(solution)/shard_map/ppermute | solution.py:106
  99.0 20.5 %collective-permute-start.2 = (bf16[64,4096]{1,0:T(8,128)(2,1)S(1)}, bf16[64,4096]{1,0:T(8,128)(2,1)S(1)}, u32[]{:S(2)}, u32[]{:S(2)}) collective-permute-start(bf16[64,4096]{1,0:T(8,128)(2,1)S(1)} %collective-permute-done), channel_id=1, source_target_pairs={{0,4},{4,8},{8,12},{12,0},{1,5},{5,9},{9,13},{13,1},{2,6},{6,10},{... | collective-permute-start | bytes 1572872 | tf_op jit(solution)/shard_map/ppermute | solution.py:101
  119.5 8.4 %copy-start.12 = (s32[64,2]{0,1:T(2,128)S(1)}, s32[64,2]{0,1:T(2,128)}, u32[]{:S(2)}) copy-start(s32[64,2]{0,1:T(2,128)} %param.29) | copy-start | bytes 1540
  119.5 31.2 %copy-start.7 = (bf16[64,1792]{1,0:T(8,128)(2,1)S(1)}, bf16[64,1792]{1,0:T(8,128)(2,1)}, u32[]{:S(2)}) copy-start(bf16[64,1792]{1,0:T(8,128)(2,1)} %param.28) | copy-start | bytes 688132
  127.9 128.3 %reduce-scatter.5.cloned.1.call-start = ((), (), s32[]{:S(2)}) async-start(), calls=%async_computation.6 | async-start | bytes 2867200 | tf_op jit(solution)/shard_map/reduce_scatter | solution.py:20
  151.8 22.4 %copy-start.4 = (bf16[64,1792]{1,0:T(8,128)(2,1)}, bf16[64,1792]{1,0:T(8,128)(2,1)S(1)}, u32[]{:S(2)}) copy-start(bf16[64,1792]{1,0:T(8,128)(2,1)S(1)} %add_convert_fusion) | copy-start | bytes 688132
  174.1 30.5 %copy-start.1 = (bf16[1,7168,256]{2,1,0:T(8,128)(2,1)S(1)}, bf16[1,7168,256]{2,1,0:T(8,128)(2,1)}, u32[]{:S(2)}) copy-start(bf16[1,7168,256]{2,1,0:T(8,128)(2,1)} %param.31) | copy-start | bytes 11010052
  204.7 2.0 copy-start.14
  206.7 2.0 copy-start.15
  210.9 48.8 %copy-start.13 = (f32[64,2]{0,1:T(2,128)S(1)}, f32[64,2]{0,1:T(2,128)}, u32[]{:S(2)}) copy-start(f32[64,2]{0,1:T(2,128)} %param.30) | copy-start | bytes 1540
  256.2 12.8 %all-to-all-start.1 = ((bf16[4,40,1792]{2,1,0:T(8,128)(2,1)}), bf16[4,40,1792]{2,1,0:T(8,128)(2,1)S(1)}, u32[]{:S(2)}, u32[]{:S(2)}) async-start(bf16[4,40,1792]{2,1,0:T(8,128)(2,1)} %reduce-scatter.5.cloned.1.call-done), calls=%async_computation.3 | async-start | bytes 1146880 | tf_op jit(solution)/shard_map/all_to_all | solution.py:23
Sparse Core Ops, SparseCore 0:
  25.6 37.1 all-gather.2
  128.0 22.6 reduce-scatter.2
  211.1 45.1 reduce-scatter.4
